TPU v7x, 32 devices: a whole 2x2x4 slice. The times are simulated.
32 devices in a mesh: freq: 4 (over y, core), stcol: 8 (over z, x).
Axes of the slice: x: 2, y: 2, z: 4, core: 2. Of those that a mesh axis runs over, the one named last changes fastest.
Arguments:
- visibilities: float32 [2, 4, 512, 1, 512], P(None, 'freq', 'stcol'), may hold values from -28.8 to 28.8
- positions: float32 [3, 1, 512], replicated, may hold values from -3 to 3
- source_lmn: float32 [3, 1024], replicated, may hold values from -0.5 to 0.5
- source_flux: float32 [1024], replicated, may hold values from 0.02 to 0.2
- cluster_map: int32 [1024], replicated, may hold values from 0 to 15, as said below
- station_order: int32 [512], replicated, may hold values from 0 to 511, each once
- penalty: float32 [16], replicated, may hold values from 9.8304 to 196.608
- offsets: float32 [2, 4, 16, 512], P(None, 'freq'), may hold values from -1.2 to 1.2
Outputs:
- gains: float32 [2, 4, 16, 512], P(None, 'freq', None, 'stcol')
- consensus: float32 [2, 4, 16, 512], P(None, 'freq', None, 'stcol')
Inputs may be any that keep to these rules, and one draw needn't show every extreme that they name: `cluster_map`: each of the 16 directions is named by exactly 64 sources. `station_order`: every station stands exactly once.
All inputs are finite; a program needn't handle non-finite values.
Results may differ from a plain program's by a relative error of at most 0.00011.
Values sent between devices are 32-bit elements; how exact they have to be, the bound alone decides.
A program may use at most 64 MiB of HBM per device.

v0:
```python
import math

import jax
import jax.numpy as jnp
from jax import lax
from jax.sharding import PartitionSpec as P

ADMM = 2
PASSES = 2


HIGHEST = lax.Precision.HIGHEST


def frequencies(channels):
    return 1.0 + 0.5 * jnp.arange(channels, dtype=jnp.float32) / channels


def basis_table(channels):
    centre = (jnp.arange(channels, dtype=jnp.float32) - 0.5 * (channels - 1)) / channels
    columns = [jnp.ones_like(centre), centre, centre * centre]
    finished = []
    for column in columns:
        for before in finished:
            column = column - jnp.sum(column * before) * before
        finished.append(column / jnp.sqrt(jnp.sum(column * column)))
    return jnp.stack(finished, axis=1)


def group_sources(source_lmn, source_flux, cluster_map, directions):
    ranking = jnp.argsort(cluster_map, stable=True)
    cosines = jnp.take(source_lmn, ranking, axis=1).reshape(3, directions, -1)
    brightness = jnp.take(source_flux, ranking).reshape(directions, -1)
    return (jnp.moveaxis(cosines, 1, 0), brightness)


def contract(row_part, column_part):
    return jnp.einsum("ctps,ctjs->cjtp", row_part, column_part, precision=HIGHEST)


def model_block(positions, direction_cosines, weights, freq_scale, column_ids):
    projected = (
        positions[0][:, :, None] * direction_cosines[0]
        + positions[1][:, :, None] * direction_cosines[1]
    )
    projected = projected + positions[2][:, :, None] * direction_cosines[2]
    phases = 2.0 * math.pi * freq_scale[:, None, None, None] * projected[None]
    cosine = jnp.cos(phases)
    sine_part = jnp.sin(phases)
    weighted_cos = cosine * weights
    weighted_sin = sine_part * weights
    column_cos = jnp.take(cosine, column_ids, axis=2)
    column_sin = jnp.take(sine_part, column_ids, axis=2)
    model_real = contract(weighted_cos, column_cos) + contract(weighted_sin, column_sin)
    model_imag = contract(weighted_sin, column_cos) - contract(weighted_cos, column_sin)
    station_ids = jnp.arange(positions.shape[2], dtype=jnp.int32)
    retained = (column_ids[:, None] != station_ids[None, :]).astype(model_real.dtype)
    retained = retained[None, :, None, :]
    return (model_real * retained, model_imag * retained)


def build_models(positions, cosines, brightness, freq_scale, column_ids):

    def one_model(entry):
        return model_block(positions, entry[0], entry[1], freq_scale, column_ids)

    return lax.map(one_model, (cosines, brightness))


def gain_update(numerator, denominator, gains, consensus, multiplier, penalty):
    weight_pen = penalty[:, None]
    scaling = 1.0 / (denominator + weight_pen)
    fresh = (numerator + gains * denominator + weight_pen * (consensus - multiplier)) * scaling
    return 0.5 * (gains + fresh)


def pass_terms(visibilities, gains, model_real, model_imag, column_ids):
    column_gains = jnp.take(gains, column_ids, axis=3)
    column_real = jnp.moveaxis(column_gains[0], 1, 0)[:, :, :, None, None]
    column_imag = jnp.moveaxis(column_gains[1], 1, 0)[:, :, :, None, None]
    row_real = jnp.moveaxis(gains[0], 1, 0)[:, :, None, None, :]
    row_imag = jnp.moveaxis(gains[1], 1, 0)[:, :, None, None, :]
    along_real = model_real * column_real + model_imag * column_imag
    along_imag = model_imag * column_real - model_real * column_imag
    pred_real = row_real * along_real - row_imag * along_imag
    pred_imag = row_real * along_imag + row_imag * along_real
    resid_real = visibilities[0] - jnp.sum(pred_real, axis=0)
    resid_imag = visibilities[1] - jnp.sum(pred_imag, axis=0)
    num_real = jnp.sum(resid_real * along_real + resid_imag * along_imag, axis=(2, 3))
    num_imag = jnp.sum(resid_imag * along_real - resid_real * along_imag, axis=(2, 3))
    denominator = jnp.sum(along_real * along_real + along_imag * along_imag, axis=(2, 3))
    numerator = jnp.moveaxis(jnp.stack([num_real, num_imag]), 1, 2)
    return (numerator, jnp.moveaxis(denominator, 0, 1)[None])


def channel_fit(values, local_basis):
    partial_sums = jnp.einsum("fj,rfkp->rjkp", local_basis, values, precision=HIGHEST)
    coefficients = lax.psum(partial_sums, "freq")
    return jnp.einsum("fj,rjkp->rfkp", local_basis, coefficients, precision=HIGHEST)


def on_device(
    visibilities, positions, source_lmn, source_flux, cluster_map, station_order, penalty, offsets
):
    chan_dev = visibilities.shape[1]
    column_count = visibilities.shape[2]
    stations = visibilities.shape[4]
    directions = penalty.shape[0]
    channels = chan_dev * lax.axis_size("freq")
    row_index = lax.axis_index("freq")
    col_index = lax.axis_index("stcol")
    owned_count = stations // lax.axis_size("stcol")
    column_ids = lax.dynamic_slice_in_dim(station_order, col_index * column_count, column_count)
    freq_scale = lax.dynamic_slice_in_dim(frequencies(channels), row_index * chan_dev, chan_dev)
    basis = basis_table(channels)
    local_basis = lax.dynamic_slice_in_dim(basis, row_index * chan_dev, chan_dev, 0)
    cosines, brightness = group_sources(source_lmn, source_flux, cluster_map, directions)
    model_real, model_imag = build_models(positions, cosines, brightness, freq_scale, column_ids)
    gains = jnp.stack([1.0 + offsets[0], offsets[1]])
    consensus = gains
    multiplier = jnp.zeros_like(gains)
    for admm_step in range(ADMM):
        for sweep_index in range(PASSES):
            numerator, denominator = pass_terms(
                visibilities, gains, model_real, model_imag, column_ids
            )
            numerator, denominator = lax.psum((numerator, denominator), "stcol")
            gains = gain_update(numerator, denominator, gains, consensus, multiplier, penalty)
        consensus = channel_fit(gains + multiplier, local_basis)
        multiplier = multiplier + gains - consensus
    gains_out = lax.dynamic_slice_in_dim(gains, col_index * owned_count, owned_count, 3)
    cons_out = lax.dynamic_slice_in_dim(consensus, col_index * owned_count, owned_count, 3)
    return (gains_out, cons_out)


def solution(mesh):
    in_specs = (
        P(None, "freq", "stcol", None, None),
        P(),
        P(),
        P(),
        P(),
        P(),
        P(),
        P(None, "freq", None, None),
    )
    out_specs = (P(None, "freq", None, "stcol"), P(None, "freq", None, "stcol"))
    return jax.shard_map(
        on_device, mesh=mesh, in_specs=in_specs, out_specs=out_specs, check_vma=False
    )
```

profile of v0, /device:TPU:0, one launch (start us, length us, event | category | flops | bytes accessed | tf_op | source)
XLA Modules:
  0.0 582.2 jit_solution(7560727911189916129)
XLA Ops:
  7.3 5.1 sort.17
  16.7 2.8 gather_fusion.2
  19.9 4.5 gather_fusion.3
  25.8 137.8 %while.14 = (s32[]{:T(128)}, f32[16,1,64,1,512]{4,2,3,1,0:T(8,128)S(1)}, f32[16,1,64,1,512]{4,2,3,1,0:T(8,128)}, s32[64]{0:T(128)S(1)}, f32[1,1,1,1]{3,2,1,0:T(1...) while((s32[]{:T(128)}, ...), condition=%wide.region_2.4_spmd, body=%wide.region_1.3_spmd.sunk | while | flops 101992000 | bytes 1256825 | solution.py:67
  29.5 2.0 fusion.98
  38.1 2.1 fusion.98
  41.6 1.4 fusion.96
  46.7 2.1 fusion.98
  50.2 1.4 fusion.96
  55.4 2.1 fusion.98
  64.0 2.1 fusion.98
  72.6 2.0 fusion.98
  76.0 1.4 fusion.96
  81.2 2.1 fusion.98
  84.6 1.4 fusion.96
  89.8 2.1 fusion.98
  93.3 1.4 fusion.96
  98.4 2.1 fusion.98
  107.0 2.1 fusion.98
  110.5 1.4 fusion.96
  115.6 2.0 fusion.98
  119.1 1.4 fusion.96
  124.3 2.1 fusion.98
  127.7 1.4 fusion.96
  132.9 2.0 fusion.98
  136.3 1.4 fusion.96
  141.5 2.1 fusion.98
  144.9 1.4 fusion.96
  150.1 2.0 fusion.98
  153.5 1.4 fusion.96
  158.7 2.1 fusion.98
  162.1 1.4 fusion.96
  163.6 2.6 subtract_reduce_fusion.7
  169.5 38.9 %psum.71 = f32[1,1,16,512]{3,2,1,0:T(8,128)S(1)} all-reduce(f32[1,1,16,512]{3,2,1,0:T(8,128)S(1)} %bitcast.261), channel_id=1, replica_groups=mesh['freq'=4,'stcol'=8] {'stcol'}, use_global_device_ids=true, to_apply=%region_9.12 | all-reduce | flops 8192 | bytes 65536 | tf_op jit(solution)/shard_map/psum | solution.py:127
  214.6 25.7 %all-reduce.7.cloned.1.call-done = f32[2,1,16,512]{3,2,1,0:T(8,128)} async-done(((f32[2,1,16,512]{3,2,1,0:T(8,128)}), f32[2,1,16,512]{3,2,1,0:T(8,128)}) %all-reduce.7.cloned.1.call-update) | async-done | bytes 65552 | tf_op jit(solution)/shard_map/psum | solution.py:127
  243.6 2.6 subtract_reduce_fusion.5
  248.1 36.2 %psum.73 = f32[1,1,16,512]{3,2,1,0:T(8,128)S(1)} all-reduce(f32[1,1,16,512]{3,2,1,0:T(8,128)S(1)} %bitcast.262), channel_id=1, replica_groups=mesh['freq'=4,'stcol'=8] {'stcol'}, use_global_device_ids=true, to_apply=%region_16.19 | all-reduce | flops 8192 | bytes 65536 | tf_op jit(solution)/shard_map/psum | solution.py:127
  284.4 33.1 %all-reduce.9.cloned.1.call-done = f32[2,1,16,512]{3,2,1,0:T(8,128)} async-done(((f32[2,1,16,512]{3,2,1,0:T(8,128)}), f32[2,1,16,512]{3,2,1,0:T(8,128)}) %all-reduce.9.cloned.1.call-update) | async-done | bytes 65552 | tf_op jit(solution)/shard_map/psum | solution.py:127
  319.8 2.6 subtract_reduce_fusion.3
  323.7 36.1 %psum.75 = f32[1,1,16,512]{3,2,1,0:T(8,128)S(1)} all-reduce(f32[1,1,16,512]{3,2,1,0:T(8,128)S(1)} %bitcast.264), channel_id=1, replica_groups=mesh['freq'=4,'stcol'=8] {'stcol'}, use_global_device_ids=true, to_apply=%region_23.26 | all-reduce | flops 8192 | bytes 65536 | tf_op jit(solution)/shard_map/psum | solution.py:127
  361.4 28.7 %all-reduce.13.cloned.1.call-done = f32[2,3,16,512]{3,2,1,0:T(8,128)} async-done(((f32[2,3,16,512]{3,2,1,0:T(8,128)}), f32[2,3,16,512]{3,2,1,0:T(8,128)}) %all-reduce.13.cloned.1.call-update) | async-done | bytes 196624 | tf_op jit(solution)/shard_map/psum | solution.py:98
  390.1 1.6 fusion.59
  391.7 71.0 %all-reduce.11.cloned.1.call-done = f32[2,1,16,512]{3,2,1,0:T(8,128)} async-done(((f32[2,1,16,512]{3,2,1,0:T(8,128)}), f32[2,1,16,512]{3,2,1,0:T(8,128)}) %all-reduce.11.cloned.1.call-update) | async-done | bytes 65552 | tf_op jit(solution)/shard_map/psum | solution.py:127
  464.9 2.6 subtract_reduce_fusion.1
  469.5 36.2 %psum.78 = f32[1,1,16,512]{3,2,1,0:T(8,128)S(1)} all-reduce(f32[1,1,16,512]{3,2,1,0:T(8,128)S(1)} %bitcast.263), channel_id=1, replica_groups=mesh['freq'=4,'stcol'=8] {'stcol'}, use_global_device_ids=true, to_apply=%region_36.39 | all-reduce | flops 8192 | bytes 65536 | tf_op jit(solution)/shard_map/psum | solution.py:127
  505.8 33.1 %all-reduce.15.cloned.1.call-done = f32[2,1,16,512]{3,2,1,0:T(8,128)} async-done(((f32[2,1,16,512]{3,2,1,0:T(8,128)}), f32[2,1,16,512]{3,2,1,0:T(8,128)}) %all-reduce.15.cloned.1.call-update) | async-done | bytes 65552 | tf_op jit(solution)/shard_map/psum | solution.py:127
  541.3 31.8 %all-reduce.17.cloned.1.call-done = f32[2,3,16,512]{3,2,1,0:T(8,128)} async-done(((f32[2,3,16,512]{3,2,1,0:T(8,128)}), f32[2,3,16,512]{3,2,1,0:T(8,128)}) %all-reduce.17.cloned.1.call-update) | async-done | bytes 196624 | tf_op jit(solution)/shard_map/psum | solution.py:98
  573.0 1.6 fusion.57
  (315 shorter events, 116.6 us)
Async XLA Ops:
  7.2 12.7 %copy-start = (f32[1024]{0:T(1024)S(1)}, f32[1024]{0:T(1024)}, u32[]{:S(2)}) copy-start(f32[1024]{0:T(1024)} %param.17) | copy-start | bytes 12292
  7.2 233.1 %all-reduce.7.cloned.1.call-start = ((), (), s32[]{:S(2)}) async-start(), calls=%async_computation | async-start | bytes 131072 | tf_op jit(solution)/shard_map/psum | solution.py:127
  13.1 0.8 copy-start.7
  13.1 1.9 copy-start.6
  19.9 5.9 %copy-start.3 = (f32[3,1,512]{2,1,0:T(1,128)S(1)}, f32[3,1,512]{2,1,0:T(1,128)}, u32[]{:S(2)}) copy-start(f32[3,1,512]{2,1,0:T(1,128)} %param.15) | copy-start | bytes 18436
  19.9 5.9 %copy-start.8 = (s32[64]{0:T(128)S(1)}, s32[64]{0:T(128)}, u32[]{:S(2)}) copy-start(s32[64]{0:T(128)} %copy-done.7) | copy-start | bytes 772
  25.8 137.8 %copy-start.5 = (f32[16,64]{1,0:T(8,128)S(1)}, f32[16,64]{1,0:T(8,128)}, u32[]{:S(2)}) copy-start(f32[16,64]{1,0:T(8,128)} %copy.125) | copy-start | bytes 12292
  163.6 2.6 copy-start.1
  166.5 47.9 %copy-start.4 = (f32[16]{0:T(128)S(1)}, f32[16]{0:T(128)}, u32[]{:S(2)}) copy-start(f32[16]{0:T(128)} %param.20) | copy-start | bytes 196
  168.1 149.4 %all-reduce.9.cloned.1.call-start = ((), (), s32[]{:S(2)}) async-start(), calls=%async_computation.1 | async-start | bytes 131072 | tf_op jit(solution)/shard_map/psum | solution.py:127
  246.4 71.1 %copy-start.2 = (f32[2,1,16,512]{3,2,1,0:T(8,128)S(1)}, f32[2,1,16,512]{3,2,1,0:T(8,128)}, u32[]{:S(2)}) copy-start(f32[2,1,16,512]{3,2,1,0:T(8,128)} %all-reduce.7.cloned.1.call-done) | copy-start | bytes 196612
  248.1 142.0 %all-reduce.13.cloned.1.call-start = ((), (), s32[]{:S(2)}) async-start(), calls=%async_computation.3 | async-start | bytes 393216 | tf_op jit(solution)/shard_map/psum | solution.py:98
  360.7 102.0 %all-reduce.11.cloned.1.call-start = ((), (), s32[]{:S(2)}) async-start(), calls=%async_computation.2 | async-start | bytes 131072 | tf_op jit(solution)/shard_map/psum | solution.py:127
  361.4 177.5 %all-reduce.15.cloned.1.call-start = ((), (), s32[]{:S(2)}) async-start(), calls=%async_computation.4 | async-start | bytes 131072 | tf_op jit(solution)/shard_map/psum | solution.py:127
  469.5 103.6 %all-reduce.17.cloned.1.call-start = ((), (), s32[]{:S(2)}) async-start(), calls=%async_computation.5 | async-start | bytes 393216 | tf_op jit(solution)/shard_map/psum | solution.py:98
Sparse Core Ops, SparseCore 0:
  168.2 72.0 all-reduce.6
  248.2 69.2 all-reduce.8
  360.8 29.2 all-reduce.12
  393.3 69.2 all-reduce.10
  469.6 69.2 all-reduce.14
  541.1 31.9 all-reduce.16
where the time goes:
time: 583 us; the launch traced here: 582 us
  waiting for transfers between devices  223 us (38%)
  blocking collectives  147 us (25%)
  matrix products  103 us (18%)
  other arithmetic  52.9 us (9%)
  local copies, waits for them, and re-layouts  35.5 us (6%)
  between operations  18 us (3%)
    psum x4, waiting for transfers between devices, on_device(): numerator, denominator = lax.psum((numerator, denominator), 'stcol')  163 us
    psum x4, blocking collectives, on_device(): numerator, denominator = lax.psum((numerator, denominator), 'stcol')  147 us
    dot_general x64, matrix products, contract(): jnp.einsum('ctps,ctjs->cjtp', row_part, column_part, precision=HIGHEST)  100 us
    psum x2, waiting for transfers between devices, channel_fit(): coefficients = lax.psum(partial_sums, 'freq')  60.4 us
    another operation x16, other arithmetic, model_block(): column_sin = jnp.take(sine_part, column_ids, axis=2)  16.5 us
  transfers between devices with their start and end apart: 6, of which 6 were waited for; matrix products, arithmetic and copies ran while one was open for 1% of the time, Pallas kernels for 0%

commit v1 on v0

v1 whole, which is shorter than its diff:
```python
import functools

import jax
import jax.numpy as jnp
import numpy as np
from jax import lax
from jax.experimental import pallas as pl
from jax.experimental.pallas import tpu as pltpu
from jax.sharding import PartitionSpec as P

ADMM = 2
PASSES = 2

F32 = jnp.float32
BF16 = jnp.bfloat16
MESH = pl.DeviceIdType.MESH

SIN_COEFS = (6.2831852802614145, -10.335420167015846, 5.1001550464297125, -1.1965825712423341, 0.15531532061178804)
COS_COEFS = (0.9999999997799043, -4.934802137078822, 4.0587091595560825, -1.335212003047854, 0.2349373138047365, -0.02439632433202294)


def basis_table(channels):
    centre = (np.arange(channels, dtype=np.float32) - np.float32(0.5 * (channels - 1))) / np.float32(
        channels
    )
    finished = []
    for column in [np.ones_like(centre), centre, centre * centre]:
        for before in finished:
            column = column - np.sum(column * before) * before
        finished.append(column / np.sqrt(np.sum(column * column)))
    return np.stack(finished, axis=1).astype(np.float32)


def poly(coefs, u):
    out = coefs[-1] * u + coefs[-2]
    for c in coefs[-3::-1]:
        out = out * u + c
    return out


def cos_sin_turns(turns):
    r = turns - jnp.round(turns)
    u = r * r
    s2 = r * poly(SIN_COEFS, u)
    c = poly(COS_COEFS, u)
    return 1.0 - 0.5 * (s2 * s2), s2 * c


def split2(x):
    hi = x.astype(BF16)
    lo = (x - hi.astype(F32)).astype(BF16)
    return hi, lo


def dot(a, b):
    return lax.dot_general(a, b, (((1,), (0,)), ((), ())), preferred_element_type=F32)


def kernel(
    sizes,
    vis_ref,
    pos_ref,
    lmn_ref,
    flux_ref,
    cmap_ref,
    order_ref,
    pen_ref,
    off_ref,
    gains_ref,
    cons_ref,
    vsend,
    vrecv,
    scol,
    model,
    vrow,
    zbuf,
    gcol,
    grow,
    nd,
    gbuf,
    fbuf,
    vs_sem,
    vr_sem,
    gs_sem,
    gr_sem,
    fs_sem,
    fr_sem,
):
    nf, ns, K, N, own, cols, S = sizes
    row = lax.axis_index("freq")
    me = lax.axis_index("stcol")
    total = K * S
    basis = basis_table(nf)

    def st_peer(i):
        return lax.rem(me + i, ns)

    def fr_peer(i):
        return lax.rem(row + i, nf)

    barrier = pltpu.get_barrier_semaphore()
    for i in range(1, ns):
        pl.semaphore_signal(barrier, inc=1, device_id={"stcol": st_peer(i)}, device_id_type=MESH)
    for i in range(1, nf):
        pl.semaphore_signal(barrier, inc=1, device_id={"freq": fr_peer(i)}, device_id_type=MESH)

    for d in range(ns):
        vsend[d] = jnp.concatenate(
            [vis_ref[0, :, d * own : (d + 1) * own], vis_ref[1, :, d * own : (d + 1) * own]], axis=1
        )
    vrecv[pl.ds(me, 1)] = vsend[pl.ds(me, 1)]
    pl.semaphore_wait(barrier, ns + nf - 2)

    vcopies = []
    for i in range(1, ns):
        peer = st_peer(i)
        copy = pltpu.make_async_remote_copy(
            src_ref=vsend.at[peer],
            dst_ref=vrecv.at[me],
            send_sem=vs_sem.at[i],
            recv_sem=vr_sem.at[i],
            device_id={"stcol": peer},
            device_id_type=MESH,
        )
        copy.start()
        vcopies.append(copy)

    def own_lanes(get):
        out = get(0)
        for d in range(1, ns):
            out = jnp.where(me == d, get(d), out)
        return out

    nu = 1.0 + 0.5 * row.astype(F32) / nf
    pos = pos_ref[...] * nu
    pos_own = own_lanes(lambda d: pos[:, d * own : (d + 1) * own])
    pos_own2 = jnp.concatenate([pos_own, pos_own], axis=1)
    lane2 = lax.broadcasted_iota(jnp.int32, (1, 2 * own), 1)
    quarter = jnp.where(lane2 >= own, 0.25, 0.0).astype(F32)
    g_re = own_lanes(lambda d: off_ref[0, :, d * own : (d + 1) * own]) + 1.0
    g_im = own_lanes(lambda d: off_ref[1, :, d * own : (d + 1) * own])

    key = cmap_ref[...].astype(F32) * total + lax.broadcasted_iota(jnp.int32, (1, total), 1).astype(F32)
    key_col = jnp.broadcast_to(key, (8, total)).T[:, 0:1]
    rank = jnp.zeros((1, total), F32)
    chunk = 128
    for b in range(0, total, chunk):
        less = jnp.where(key_col[b : b + chunk] < key, 1.0, 0.0)
        rank = rank + jnp.sum(less, axis=0, keepdims=True)
    attr = jnp.concatenate([lmn_ref[...], flux_ref[...]], axis=0)
    a_hi = attr.astype(BF16).astype(F32)
    a_mid = (attr - a_hi).astype(BF16).astype(F32)
    a_lo = attr - a_hi - a_mid
    stacked = jnp.concatenate([a_hi, a_mid, a_lo, jnp.zeros((116, total), F32)], axis=0)
    attr_t = stacked.T.astype(BF16)
    step = min(256, total)

    def sort_body(b, carry):
        slot = lax.broadcasted_iota(jnp.int32, (step, total), 0) + b * step
        pick = jnp.where(slot.astype(F32) == rank, 1.0, 0.0).astype(BF16)
        got = dot(pick, attr_t)
        scol[pl.ds(pl.multiple_of(b * step, step), step), :] = (
            got + pltpu.roll(got, 124, 1) + pltpu.roll(got, 120, 1)
        )
        return carry

    lax.fori_loop(0, total // step, sort_body, 0)

    diag_rows = lax.rem(lax.broadcasted_iota(jnp.int32, (2 * own, N), 0), own) + me * own
    diag = diag_rows == lax.broadcasted_iota(jnp.int32, (2 * own, N), 1)

    def model_body(k, carry):
        src = scol[pl.ds(pl.multiple_of(k * S, S), S), :]
        sl, sm, sn, w = src[:, 0:1], src[:, 1:2], src[:, 2:3], src[:, 3:4]
        t_all = sl * pos[0:1] + sm * pos[1:2] + sn * pos[2:3]
        c_all, s_all = cos_sin_turns(t_all)
        t_own = sl * pos_own2[0:1] + sm * pos_own2[1:2] + sn * pos_own2[2:3] - quarter
        c_own, s_own = cos_sin_turns(t_own)
        left = jnp.concatenate([c_own * w, s_own * w], axis=0).T
        l_hi, l_lo = split2(left)
        r_hi, r_lo = split2(jnp.concatenate([c_all, s_all], axis=0))
        m = dot(jnp.concatenate([l_hi, l_lo, l_hi], axis=1), jnp.concatenate([r_hi, r_hi, r_lo], axis=0))
        model[k] = jnp.where(diag, 0.0, m)
        return carry

    lax.fori_loop(0, K, model_body, 0)

    for copy in vcopies:
        copy.wait()
    place = lax.broadcasted_iota(jnp.int32, (N, N), 0) == order_ref[...]
    place = jnp.where(place, 1.0, 0.0).astype(BF16)
    v_hi, v_lo = split2(vrecv[...].reshape(N, 2 * own))
    got = dot(place, v_hi) + dot(place, v_lo)
    vrow[...] = got.T

    pen = pen_ref[...]
    lane = lax.broadcasted_iota(jnp.int32, (8, 128), 1)

    def set_rows(re, im):
        both = jnp.concatenate([re, im], axis=0)
        grow[:, : 2 * K] = both.T

    def terms():
        def body(i, carry):
            up = pl.ds(pl.multiple_of(8 * i, 8), 8)
            down = pl.ds(pl.multiple_of(own + 8 * i, 8), 8)
            res_r = vrow[up, :]
            res_i = vrow[down, :]
            row_g = grow[up, :]
            out = jnp.zeros((8, 128), F32)
            for k in range(K):
                mr = model[k, up, :]
                mi = model[k, down, :]
                cr = gcol[k : k + 1, :]
                ci = gcol[K + k : K + k + 1, :]
                zr = mr * cr + mi * ci
                zi = mi * cr - mr * ci
                zbuf[k, 0:8] = zr
                zbuf[k, 8:16] = zi
                rr = row_g[:, k : k + 1]
                ri = row_g[:, K + k : K + k + 1]
                res_r = res_r - (rr * zr - ri * zi)
                res_i = res_i - (rr * zi + ri * zr)
                dn = jnp.sum(zr * zr + zi * zi, axis=1, keepdims=True)
                out = jnp.where(lane == 2 * K + k, dn, out)
            for k in range(K):
                zr = zbuf[k, 0:8]
                zi = zbuf[k, 8:16]
                nr = jnp.sum(res_r * zr + res_i * zi, axis=1, keepdims=True)
                ni = jnp.sum(res_i * zr - res_r * zi, axis=1, keepdims=True)
                out = jnp.where(lane == k, nr, out)
                out = jnp.where(lane == K + k, ni, out)
            nd[up, :] = out
            return carry

        lax.fori_loop(0, own // 8, body, 0)
        flipped = nd[...].T
        return flipped[0:K], flipped[K : 2 * K], flipped[2 * K : 3 * K]

    def exchange(buf, stage, count, mine, name, peer_of, send_sem, recv_sem, block):
        buf[stage, pl.ds(mine, 1)] = block[None]
        copies = []
        for i in range(1, count):
            copy = pltpu.make_async_remote_copy(
                src_ref=buf.at[stage, mine],
                dst_ref=buf.at[stage, mine],
                send_sem=send_sem.at[stage, i],
                recv_sem=recv_sem.at[stage, i],
                device_id={name: peer_of(i)},
                device_id_type=MESH,
            )
            copy.start()
            copies.append(copy)
        return copies

    def fit(step, re, im):
        b_row = [
            functools.reduce(
                lambda acc, f: jnp.where(row == f, float(basis[f, j]), acc), range(1, nf), float(basis[0, j])
            )
            for j in range(3)
        ]
        out = None
        for j in range(3):
            coef = float(basis[0, j]) * fbuf[step, 0]
            for f in range(1, nf):
                coef = coef + float(basis[f, j]) * fbuf[step, f]
            part = b_row[j] * coef
            out = part if out is None else out + part
        return out[:, :own], out[:, own:]

    gcol[0:K, :] = off_ref[0] + 1.0
    gcol[K : 2 * K, :] = off_ref[1]
    grow[...] = jnp.zeros_like(grow)
    set_rows(g_re, g_im)
    c_re, c_im = g_re, g_im
    d_re = d_im = jnp.zeros_like(g_re)
    fit_copies = None
    stage = 0
    for admm in range(ADMM):
        for sweep in range(PASSES):
            nr, ni, dn = terms()
            if fit_copies is not None:
                for copy in fit_copies:
                    copy.wait()
                fit_copies = None
                c_re, c_im = fit(admm - 1, None, None)
                d_re = d_re + g_re - c_re
                d_im = d_im + g_im - c_im
            scaling = 1.0 / (dn + pen)
            f_re = (nr + g_re * dn + pen * (c_re - d_re)) * scaling
            f_im = (ni + g_im * dn + pen * (c_im - d_im)) * scaling
            g_re = 0.5 * (g_re + f_re)
            g_im = 0.5 * (g_im + f_im)
            last = admm == ADMM - 1 and sweep == PASSES - 1
            if not last:
                copies = exchange(
                    gbuf, stage, ns, me, "stcol", st_peer, gs_sem, gr_sem,
                    jnp.concatenate([g_re, g_im], axis=1),
                )
            if sweep == PASSES - 1:
                fit_copies = exchange(
                    fbuf, admm, nf, row, "freq", fr_peer, fs_sem, fr_sem,
                    jnp.concatenate([g_re + d_re, g_im + d_im], axis=1),
                )
            if not last:
                set_rows(g_re, g_im)
                for copy in copies:
                    copy.wait()
                gcol[0:K, :] = jnp.concatenate([gbuf[stage, d][:, :own] for d in range(ns)], axis=1)
                gcol[K : 2 * K, :] = jnp.concatenate([gbuf[stage, d][:, own:] for d in range(ns)], axis=1)
                stage += 1
    gains_ref[0] = g_re
    gains_ref[1] = g_im
    for copy in fit_copies:
        copy.wait()
    c_re, c_im = fit(ADMM - 1, None, None)
    cons_ref[0] = c_re
    cons_ref[1] = c_im


def on_device(
    visibilities, positions, source_lmn, source_flux, cluster_map, station_order, penalty, offsets
):
    nf = lax.axis_size("freq")
    ns = lax.axis_size("stcol")
    cols = visibilities.shape[2]
    N = visibilities.shape[4]
    K = penalty.shape[0]
    total = source_flux.shape[0]
    S = total // K
    own = N // ns
    assert visibilities.shape[1] == 1 and visibilities.shape[3] == 1
    exchanges = ADMM * PASSES - 1
    vmem = pl.BlockSpec(memory_space=pltpu.VMEM)
    shape = jax.ShapeDtypeStruct((2, K, own), F32)
    dma = pltpu.SemaphoreType.DMA
    gains, cons = pl.pallas_call(
        functools.partial(kernel, (nf, ns, K, N, own, cols, S)),
        out_shape=(shape, shape),
        in_specs=[vmem] * 8,
        out_specs=(vmem, vmem),
        scratch_shapes=[
            pltpu.VMEM((ns, cols, 2 * own), F32),
            pltpu.VMEM((ns, cols, 2 * own), F32),
            pltpu.VMEM((total, 128), F32),
            pltpu.VMEM((K, 2 * own, N), F32),
            pltpu.VMEM((2 * own, N), F32),
            pltpu.VMEM((K, 16, N), F32),
            pltpu.VMEM((2 * K, N), F32),
            pltpu.VMEM((own, 128), F32),
            pltpu.VMEM((own, 128), F32),
            pltpu.VMEM((exchanges, ns, K, 2 * own), F32),
            pltpu.VMEM((ADMM, nf, K, 2 * own), F32),
            dma((ns,)),
            dma((ns,)),
            dma((exchanges, ns)),
            dma((exchanges, ns)),
            dma((ADMM, nf)),
            dma((ADMM, nf)),
        ],
        compiler_params=pltpu.CompilerParams(collective_id=0, has_side_effects=True),
        name="calibrate",
    )(
        visibilities.reshape(2, cols, N),
        positions.reshape(3, N),
        source_lmn,
        source_flux.reshape(1, total),
        cluster_map.reshape(1, total),
        station_order.reshape(1, N),
        penalty.reshape(K, 1),
        offsets.reshape(2, K, N),
    )
    return gains[:, None], cons[:, None]


def solution(mesh):
    in_specs = (
        P(None, "freq", "stcol", None, None),
        P(),
        P(),
        P(),
        P(),
        P(),
        P(),
        P(None, "freq", None, None),
    )
    out_specs = (P(None, "freq", None, "stcol"), P(None, "freq", None, "stcol"))
    return jax.shard_map(
        on_device, mesh=mesh, in_specs=in_specs, out_specs=out_specs, check_vma=False
    )
```

time: 583 us -> 57.7 us (0.10)
  waiting for transfers between devices: 223 us -> 0 us
  blocking collectives: 147 us -> 0 us
  matrix products: 103 us -> 0 us
  other arithmetic: 52.9 us -> 0 us
  Pallas kernels: 0 us -> 50.6 us
  local copies, waits for them, and re-layouts: 35.5 us -> 6.21 us
  between operations: 18 us -> 0.66 us
    psum x6 -> x0, waiting for transfers between devices: 223 us -> none  [the longest x4 163 us: on_device(): numerator, denominator = lax.psum((numerator, denominator), 'stcol')]
    psum x4 -> x0, blocking collectives: 147 us -> none  [on_device(): numerator, denominator = lax.psum((numerator, denominator), 'stcol')]
    dot_general x66 -> x0, matrix products: 103 us -> none  [the longest x64 100 us: contract(): jnp.einsum('ctps,ctjs->cjtp', row_part, column_part, precision=HIGHEST)]
    pallas_call x0 -> x1, Pallas kernels: none -> 50.6 us  [on_device(): pl.pallas_call(functools.partial(kernel, (nf, ns, K, N, own, cols, S)), o...]
    gather x40 -> x0, local copies, waits for them, and re-layouts: 29.8 us -> none  [the longest x16 9.59 us: model_block(): column_sin = jnp.take(sine_part, column_ids, axis=2)]
    another operation x24 -> x0, other arithmetic: 18.4 us -> none  [the longest x16 16.5 us: model_block(): column_sin = jnp.take(sine_part, column_ids, axis=2)]
    reduce_sum x13 -> x0, other arithmetic: 18.1 us -> none  [the longest x4 10.3 us: pass_terms(): resid_real = visibilities[0] - jnp.sum(pred_real, axis=0)]
  transfers between devices with their start and end apart: 6 -> 0, of which waited for: 6 -> 0; matrix products, arithmetic and copies ran while one was open for 1% -> 0% of each run, Pallas kernels for 0% -> 0%
where the time goes in v1:
time: 57.7 us; the launch traced here: 57.5 us
  Pallas kernels  50.6 us (88%)
  local copies, waits for them, and re-layouts  6.21 us (11%)
  between operations  0.66 us (1%)
    pallas_call x1, Pallas kernels, on_device(): pl.pallas_call(functools.partial(kernel, (nf, ns, K, N, own, cols, S)), o...  50.6 us
    unnamed x10, local copies, waits for them, and re-layouts  5.54 us

profile of v1, /device:TPU:0, one launch (start us, length us, event | category | flops | bytes accessed | tf_op | source)
XLA Modules:
  0.0 57.5 jit_solution(6029359875358024655)
XLA Ops:
  0.6 0.0 copy-start.1
  0.6 0.7 %copy-done.1 = f32[3,1,512]{2,1,0:T(1,128)S(1)} copy-done((f32[3,1,512]{2,1,0:T(1,128)S(1)}, f32[3,1,512]{2,1,0:T(1,128)}, u32[]{:S(2)}) %copy-start.1) | copy-done | bytes 6168
  1.3 0.6 %copy.18 = f32[3,1,512]{2,0,1:T(4,128)} copy(f32[3,1,512]{2,1,0:T(1,128)S(1)} %copy-done.1) | data formatting | bytes 12288
  1.9 0.0 copy-start.2
  1.9 0.7 %copy-done.2 = f32[16]{0:T(128)S(1)} copy-done((f32[16]{0:T(128)S(1)}, f32[16]{0:T(128)}, u32[]{:S(2)}) %copy-start.2) | copy-done | bytes 88
  2.6 0.7 %copy.10.pen_ref = f32[16,1]{1,0:T(8,128)} copy(f32[16,1]{0,1:T(1,128)S(1)} %bitcast.25) | data formatting | bytes 128 | tf_op jit(solution)/shard_map/reshape | solution.py:371
  3.3 1.7 %copy.17 = f32[2,1,64,1,512]{4,2,3,1,0:T(8,128)} copy(f32[2,1,64,1,512]{4,3,2,1,0:T(1,128)} %param.8) | data formatting | bytes 524288
  4.9 50.6 %calibrate.1 = (f32[2,16,64]{2,1,0:T(8,128)}, f32[2,16,64]{2,1,0:T(8,128)}) custom-call(f32[2,64,512]{2,1,0:T(8,128)} %bitcast.17, f32[3,512]{1,0:T(4,128)} %bitcast.19, f32[3,1024]{1,0:T(4,128)} %lmn_ref.1, f32[1,1024]{1,0:T(1,128)} %bitcast.22, s32[1,1024]{1,0:T(1,128)} %bitcast.23, s32[1,512]{1,0:T(1,128)} %bitcast.24, f32[16,1]{1,0:T(8,128)} %copy.10.pen_ref, ...), custom_call_target="tpu_custom_call" | custom-call | tf_op jit(solution)/shard_map/calibrate/pallas_call | solution.py:338
  55.5 0.0 copy-start
  55.5 1.3 %copy.21 = f32[2,1,16,64]{3,2,1,0:T(8,128)} copy(f32[2,1,16,64]{3,2,1,0:T(8,128)} %bitcast.21) | data formatting | bytes 16384
  56.9 0.0 copy-done
  56.9 0.6 %copy.22 = f32[2,1,16,64]{3,2,1,0:T(8,128)} copy(f32[2,1,16,64]{3,2,1,0:T(8,128)S(1)} %bitcast.20) | data formatting | bytes 16384
Async XLA Ops:
  0.6 0.7 %copy-start.1 = (f32[3,1,512]{2,1,0:T(1,128)S(1)}, f32[3,1,512]{2,1,0:T(1,128)}, u32[]{:S(2)}) copy-start(f32[3,1,512]{2,1,0:T(1,128)} %param.9) | copy-start | bytes 18436
  1.9 0.7 %copy-start.2 = (f32[16]{0:T(128)S(1)}, f32[16]{0:T(128)}, u32[]{:S(2)}) copy-start(f32[16]{0:T(128)} %param.14) | copy-start | bytes 196
  55.5 1.3 %copy-start = (f32[2,16,64]{2,1,0:T(8,128)S(1)}, f32[2,16,64]{2,1,0:T(8,128)}, u32[]{:S(2)}) copy-start(f32[2,16,64]{2,1,0:T(8,128)} %get-tuple-element.5) | copy-start | bytes 24580

commit v2 on v1

--- a/solution.py
+++ b/solution.py
@@ -15,8 +15,8 @@
 BF16 = jnp.bfloat16
 MESH = pl.DeviceIdType.MESH
 
-SIN_COEFS = (6.2831852802614145, -10.335420167015846, 5.1001550464297125, -1.1965825712423341, 0.15531532061178804)
-COS_COEFS = (0.9999999997799043, -4.934802137078822, 4.0587091595560825, -1.335212003047854, 0.2349373138047365, -0.02439632433202294)
+SIN_COEFS = (4.442882919124344, -7.308245686509103, 3.6063542184332404, -0.8461116503750895, 0.10982451642675807)
+COS_COEFS = (1.414213496255229, -6.978850948563844, 5.739460376907473, -1.883557905987641, 0.31068802752730623)
 
 
 def basis_table(channels):
@@ -43,7 +43,7 @@
     u = r * r
     s2 = r * poly(SIN_COEFS, u)
     c = poly(COS_COEFS, u)
-    return 1.0 - 0.5 * (s2 * s2), s2 * c
+    return 1.0 - s2 * s2, s2 * c
 
 
 def split2(x):
@@ -66,8 +66,7 @@
     order_ref,
     pen_ref,
     off_ref,
-    gains_ref,
-    cons_ref,
+    out_ref,
     vsend,
     vrecv,
     scol,
@@ -104,10 +103,13 @@
     for i in range(1, nf):
         pl.semaphore_signal(barrier, inc=1, device_id={"freq": fr_peer(i)}, device_id_type=MESH)
 
+    per = N // 128
+    tiles = [
+        [vis_ref[pl.ds(r * cols * per + t, cols, stride=per), :] for t in range(per)] for r in range(2)
+    ]
     for d in range(ns):
-        vsend[d] = jnp.concatenate(
-            [vis_ref[0, :, d * own : (d + 1) * own], vis_ref[1, :, d * own : (d + 1) * own]], axis=1
-        )
+        tile, at = divmod(d * own, 128)
+        vsend[d] = jnp.concatenate([tiles[0][tile][:, at : at + own], tiles[1][tile][:, at : at + own]], axis=1)
     vrecv[pl.ds(me, 1)] = vsend[pl.ds(me, 1)]
     pl.semaphore_wait(barrier, ns + nf - 2)
 
@@ -132,7 +134,7 @@
         return out
 
     nu = 1.0 + 0.5 * row.astype(F32) / nf
-    pos = pos_ref[...] * nu
+    pos = pos_ref[:, 0, :] * nu
     pos_own = own_lanes(lambda d: pos[:, d * own : (d + 1) * own])
     pos_own2 = jnp.concatenate([pos_own, pos_own], axis=1)
     lane2 = lax.broadcasted_iota(jnp.int32, (1, 2 * own), 1)
@@ -140,38 +142,42 @@
     g_re = own_lanes(lambda d: off_ref[0, :, d * own : (d + 1) * own]) + 1.0
     g_im = own_lanes(lambda d: off_ref[1, :, d * own : (d + 1) * own])
 
-    key = cmap_ref[...].astype(F32) * total + lax.broadcasted_iota(jnp.int32, (1, total), 1).astype(F32)
-    key_col = jnp.broadcast_to(key, (8, total)).T[:, 0:1]
-    rank = jnp.zeros((1, total), F32)
-    chunk = 128
-    for b in range(0, total, chunk):
-        less = jnp.where(key_col[b : b + chunk] < key, 1.0, 0.0)
-        rank = rank + jnp.sum(less, axis=0, keepdims=True)
+    cmap = cmap_ref[...]
+    member = jnp.where(lax.broadcasted_iota(jnp.int32, (K, total), 0) == cmap, 1.0, 0.0)
+    before = jnp.where(
+        lax.broadcasted_iota(jnp.int32, (128, 128), 0) < lax.broadcasted_iota(jnp.int32, (128, 128), 1), 1.0, 0.0
+    ).astype(BF16)
+    seen = jnp.zeros((K, 1), F32)
+    places = []
+    for b in range(0, total, 128):
+        part = member[:, b : b + 128]
+        count = dot(part.astype(BF16), before) + seen
+        places.append(jnp.sum(count * part, axis=0, keepdims=True))
+        seen = seen + jnp.sum(part, axis=1, keepdims=True)
+    place_row = jnp.concatenate(places, axis=1)
+    pick = jnp.where(
+        lax.broadcasted_iota(jnp.int32, (S, total), 0).astype(F32) == place_row, 1.0, 0.0
+    ).astype(BF16)
     attr = jnp.concatenate([lmn_ref[...], flux_ref[...]], axis=0)
     a_hi = attr.astype(BF16).astype(F32)
     a_mid = (attr - a_hi).astype(BF16).astype(F32)
     a_lo = attr - a_hi - a_mid
-    stacked = jnp.concatenate([a_hi, a_mid, a_lo, jnp.zeros((116, total), F32)], axis=0)
-    attr_t = stacked.T.astype(BF16)
-    step = min(256, total)
-
-    def sort_body(b, carry):
-        slot = lax.broadcasted_iota(jnp.int32, (step, total), 0) + b * step
-        pick = jnp.where(slot.astype(F32) == rank, 1.0, 0.0).astype(BF16)
-        got = dot(pick, attr_t)
-        scol[pl.ds(pl.multiple_of(b * step, step), step), :] = (
-            got + pltpu.roll(got, 124, 1) + pltpu.roll(got, 120, 1)
+    got = jnp.zeros((S, 128), F32)
+    for part in (a_hi, a_mid, a_lo):
+        spread = jnp.concatenate(
+            [member * part[a : a + 1] for a in range(4)] + [jnp.zeros((128 - 4 * K, total), F32)], axis=0
+        ).astype(BF16)
+        got = got + lax.dot_general(
+            pick, spread, (((1,), (1,)), ((), ())), preferred_element_type=F32
         )
-        return carry
-
-    lax.fori_loop(0, total // step, sort_body, 0)
+    scol[...] = got
 
     diag_rows = lax.rem(lax.broadcasted_iota(jnp.int32, (2 * own, N), 0), own) + me * own
     diag = diag_rows == lax.broadcasted_iota(jnp.int32, (2 * own, N), 1)
 
     def model_body(k, carry):
-        src = scol[pl.ds(pl.multiple_of(k * S, S), S), :]
-        sl, sm, sn, w = src[:, 0:1], src[:, 1:2], src[:, 2:3], src[:, 3:4]
+        src = pltpu.roll(scol[...], 128 - k, 1)
+        sl, sm, sn, w = (src[:, a * K : a * K + 1] for a in range(4))
         t_all = sl * pos[0:1] + sm * pos[1:2] + sn * pos[2:3]
         c_all, s_all = cos_sin_turns(t_all)
         t_own = sl * pos_own2[0:1] + sm * pos_own2[1:2] + sn * pos_own2[2:3] - quarter
@@ -193,7 +199,7 @@
     got = dot(place, v_hi) + dot(place, v_lo)
     vrow[...] = got.T
 
-    pen = pen_ref[...]
+    pen = jnp.broadcast_to(pen_ref[...], (8, K)).T[:, 0:1]
     lane = lax.broadcasted_iota(jnp.int32, (8, 128), 1)
 
     def set_rows(re, im):
@@ -310,13 +316,18 @@
                 gcol[0:K, :] = jnp.concatenate([gbuf[stage, d][:, :own] for d in range(ns)], axis=1)
                 gcol[K : 2 * K, :] = jnp.concatenate([gbuf[stage, d][:, own:] for d in range(ns)], axis=1)
                 stage += 1
-    gains_ref[0] = g_re
-    gains_ref[1] = g_im
+    out_ref[0, 0] = g_re
+    out_ref[0, 1] = g_im
     for copy in fit_copies:
         copy.wait()
     c_re, c_im = fit(ADMM - 1, None, None)
-    cons_ref[0] = c_re
-    cons_ref[1] = c_im
+    out_ref[1, 0] = c_re
+    out_ref[1, 1] = c_im
+
+
+def hand_out(both_ref, gains_ref, cons_ref):
+    gains_ref[...] = both_ref[0]
+    cons_ref[...] = both_ref[1]
 
 
 def on_device(
@@ -335,15 +346,15 @@
     vmem = pl.BlockSpec(memory_space=pltpu.VMEM)
     shape = jax.ShapeDtypeStruct((2, K, own), F32)
     dma = pltpu.SemaphoreType.DMA
-    gains, cons = pl.pallas_call(
+    both = pl.pallas_call(
         functools.partial(kernel, (nf, ns, K, N, own, cols, S)),
-        out_shape=(shape, shape),
+        out_shape=jax.ShapeDtypeStruct((2, 2, K, own), F32),
         in_specs=[vmem] * 8,
-        out_specs=(vmem, vmem),
+        out_specs=vmem,
         scratch_shapes=[
             pltpu.VMEM((ns, cols, 2 * own), F32),
             pltpu.VMEM((ns, cols, 2 * own), F32),
-            pltpu.VMEM((total, 128), F32),
+            pltpu.VMEM((S, 128), F32),
             pltpu.VMEM((K, 2 * own, N), F32),
             pltpu.VMEM((2 * own, N), F32),
             pltpu.VMEM((K, 16, N), F32),
@@ -362,15 +373,18 @@
         compiler_params=pltpu.CompilerParams(collective_id=0, has_side_effects=True),
         name="calibrate",
     )(
-        visibilities.reshape(2, cols, N),
-        positions.reshape(3, N),
+        visibilities.reshape(-1, 128),
+        positions,
         source_lmn,
         source_flux.reshape(1, total),
         cluster_map.reshape(1, total),
         station_order.reshape(1, N),
-        penalty.reshape(K, 1),
+        penalty.reshape(1, K),
         offsets.reshape(2, K, N),
     )
+    gains, cons = pl.pallas_call(
+        hand_out, out_shape=(shape, shape), in_specs=[vmem], out_specs=(vmem, vmem), name="hand_out"
+    )(both)
     return gains[:, None], cons[:, None]
 
 

time: 57.7 us -> 51.9 us (0.90)
  local copies, waits for them, and re-layouts: 6.21 us -> 0 us
    unnamed x10 -> x0, local copies, waits for them, and re-layouts: 5.54 us -> none
    pallas_call x0 -> x1, Pallas kernels: none -> 1.37 us  [on_device(): pl.pallas_call(hand_out, out_shape=(shape, shape), in_specs=[vmem], out_s...]
    pallas_call x1, Pallas kernels: 50.6 us -> 49.7 us  [on_device(): pl.pallas_call(functools.partial(kernel, (nf, ns, K, N, own, cols, S)), o...]
    reshape x1 -> x0, local copies, waits for them, and re-layouts: 0.68 us -> none  [on_device(): penalty.reshape(K, 1)]
where the time goes in v2:
time: 51.9 us; the launch traced here: 51.7 us
  Pallas kernels  51 us (98%)
  between operations  0.64 us (1%)
    pallas_call x1, Pallas kernels, on_device(): pl.pallas_call(functools.partial(kernel, (nf, ns, K, N, own, cols, S)), o...  49.7 us
    pallas_call x1, Pallas kernels, on_device(): pl.pallas_call(hand_out, out_shape=(shape, shape), in_specs=[vmem], out_s...  1.37 us

profile of v2, /device:TPU:0, one launch (start us, length us, event | category | flops | bytes accessed | tf_op | source)
XLA Modules:
  0.0 51.7 jit_solution(15002072084455849794)
XLA Ops:
  0.6 49.7 %calibrate.1.both_ref = f32[2,2,16,64]{3,2,1,0:T(8,128)} custom-call(f32[512,128]{1,0:T(8,128)} %bitcast.12, f32[3,1,512]{2,1,0:T(1,128)} %pos_ref.1, f32[3,1024]{1,0:T(4,128)} %lmn_ref.1, f32[1,1024]{1,0:T(1,128)} %bitcast.14, s32[1,1024]{1,0:T(1,128)} %bitcast.15, s32[1,512]{1,0:T(1,128)} %bitcast.16, f32[1,16]{1,0:T(1,128)} %bitcast.17, ...), custom_call_target="tpu_custom_call" | custom-call | tf_op jit(solution)/shard_map/calibrate/pallas_call | solution.py:349
  50.3 1.4 %hand_out.1 = (f32[2,16,64]{2,1,0:T(8,128)}, f32[2,16,64]{2,1,0:T(8,128)}) custom-call(f32[2,2,16,64]{3,2,1,0:T(8,128)} %calibrate.1.both_ref), custom_call_target="tpu_custom_call" | custom-call | tf_op jit(solution)/shard_map/hand_out/pallas_call | solution.py:385
